TPU v7x, 256 devices: a whole 4x4x8 slice. The times are simulated.
256 devices in a mesh: view: 16 (over z, core), blk: 16 (over y, x).
Axes of the slice: x: 4, y: 4, z: 8, core: 2. Of those that a mesh axis runs over, the one named last changes fastest.
Arguments:
- estimate: float32 [256, 128, 128], P('blk'), may hold values from 0.5 to 2
- images: bfloat16 [16, 256, 64, 128], P('view', 'blk'), may hold values from 0.5 to 2
- point_spread: float32 [8, 9, 7, 25], replicated, may hold values from 0.01 to 1
- covered: int32 [8, 16, 4], P(None, 'blk'), may hold values from 0 to 1, as said below
Outputs:
- estimate_next: float32 [256, 128, 128], P('blk')
Inputs may be any that keep to these rules, and one draw needn't show every extreme that they name: For each view and each block layer along the first dimension, the covered blocks are consecutive along the second dimension and at most 3; for every view some block layer has exactly 3.
All inputs are finite; a program needn't handle non-finite values.
Results may differ from a plain program's by a relative error of at most 0.0003.
Values may be sent and summed in bfloat16 or wider, within the bound.
A program may use at most 64 MiB of HBM per device.

v0:
```python
import jax
import jax.numpy as jnp
from jax import lax
from jax.sharding import PartitionSpec as P

BY = 32


def with_halo(cells, sides, width):
    for axis, dim in sides:
        count = lax.axis_size(axis)
        ends = count - 1
        head = lax.slice_in_dim(cells, 0, width, axis=dim)
        tail = lax.slice_in_dim(cells, cells.shape[dim] - width, cells.shape[dim], axis=dim)
        cells = jnp.concatenate(
            [
                lax.ppermute(tail, axis, [(i, (i + 1) % count) for i in range(ends)]),
                cells,
                lax.ppermute(head, axis, [((i + 1) % count, i) for i in range(ends)]),
            ],
            axis=dim,
        )
    return cells


def swapped(block, axis, stride):
    count = lax.axis_size(axis)
    route = []
    for low in range(count):
        high = low | 1 << stride
        if high != low and high < count:
            route += [(low, high), (high, low)]
    return lax.ppermute(block, axis, route)


def merged(part, axis, combine):
    gathered = lax.all_gather(part, axis)

    def take(source):
        return lax.dynamic_index_in_dim(gathered, source, 0, False)

    return lax.fori_loop(
        1, lax.axis_size(axis), lambda source, state: combine(state, take(source)), take(0)
    )


def band_table(kernel, depth):
    taps_x, taps_y, taps_z = kernel.shape
    span_z = depth + taps_z - 1
    shape_three = (taps_z, span_z, depth)
    offset = lax.broadcasted_iota(jnp.int32, shape_three, 1) - lax.broadcasted_iota(
        jnp.int32, shape_three, 2
    )
    onehot = (offset == lax.broadcasted_iota(jnp.int32, shape_three, 0)).astype(jnp.bfloat16)
    banded = jnp.einsum("abt,tpz->abpz", kernel, onehot, preferred_element_type=jnp.float32).astype(
        jnp.bfloat16
    )
    inner_width = taps_y * span_z
    padded_width = -(-inner_width // 128) * 128
    banded = banded.reshape(taps_x, inner_width, depth)
    return jnp.pad(banded, ((0, 0), (0, padded_width - inner_width), (0, 0)))


def convolve(padded_part, banded, rows_x, rows_y):
    taps_x = padded_part.shape[0] - rows_x + 1
    taps_y = padded_part.shape[1] - rows_y + 1
    columns = jnp.concatenate(
        [padded_part[:, step_y : step_y + rows_y, :] for step_y in range(taps_y)], axis=2
    )
    columns = jnp.pad(columns, ((0, 0), (0, 0), (0, banded.shape[1] - columns.shape[2])))
    output = None
    for shift_x in range(taps_x):
        partial_sum = jnp.dot(
            columns[shift_x : shift_x + rows_x].reshape(rows_x * rows_y, -1),
            banded[shift_x],
            preferred_element_type=jnp.float32,
        )
        output = partial_sum if output is None else output + partial_sum
    return output.reshape(rows_x, rows_y, -1)


def local(estimate, images, point_spread, covered):
    slab_x, width_y, depth = estimate.shape
    share_w = images.shape[2]
    view_count, taps_x, taps_y, taps_z = point_spread.shape
    rim_x, rim_y, rim_z = ((taps_x - 1) // 2, (taps_y - 1) // 2, (taps_z - 1) // 2)
    shares = width_y // share_w
    share_blocks = share_w // BY
    group = lax.axis_index("view")
    view_id = group // shares
    part = group % shares
    y_start = part * share_w
    source = estimate.astype(jnp.bfloat16)
    rimmed = with_halo(source, (("blk", 0),), rim_x)
    padded = jnp.pad(rimmed, ((0, 0), (rim_y, rim_y), (rim_z, rim_z)))
    spread = lax.dynamic_index_in_dim(point_spread, view_id, 0, keepdims=False)
    kernel = (spread / jnp.sum(spread)).astype(jnp.bfloat16)
    forward = band_table(kernel, depth)
    backward = band_table(kernel[::-1, ::-1, ::-1], depth)
    coverage_row = lax.dynamic_index_in_dim(covered[:, 0, :], view_id, 0, keepdims=False) > 0
    share_cover = lax.dynamic_slice_in_dim(coverage_row, part * share_blocks, share_blocks)
    cell_cover = jnp.repeat(share_cover, BY)[None, :, None]
    image = images[0]
    region = lax.dynamic_slice(
        padded, (0, y_start, 0), (slab_x + 2 * rim_x, share_w + 2 * rim_y, depth + 2 * rim_z)
    )
    blurred = convolve(region, forward, slab_x, share_w)
    quotient = jnp.where(cell_cover, image.astype(jnp.float32) / blurred, 0.0).astype(jnp.bfloat16)
    rim_zeros = jnp.zeros((slab_x, rim_y, depth), jnp.bfloat16)
    edge_rows = jnp.where(part == 0, quotient[:, share_w - rim_y :, :], quotient[:, :rim_y, :])
    partner = swapped(edge_rows, "view", 0)
    lower_rim = jnp.where(part > 0, partner, rim_zeros)
    upper_rim = jnp.where(part < shares - 1, partner, rim_zeros)
    extended = jnp.concatenate([lower_rim, quotient, upper_rim], axis=1)
    quotient_rimmed = with_halo(extended, (("blk", 0),), rim_x)
    padded_quotient = jnp.pad(quotient_rimmed, ((0, 0), (0, 0), (rim_z, rim_z)))
    correction = convolve(padded_quotient, backward, slab_x, share_w)
    share_factor = jnp.where(cell_cover, correction, 1.0)
    n_view = lax.axis_size("view")
    step_x = slab_x // n_view
    rows = share_factor.reshape(n_view, step_x, share_w, depth)
    got = lax.all_to_all(rows, "view", 0, 0)
    got = got.reshape(n_view // shares, shares, step_x, share_w, depth)
    product_rows = jnp.prod(got, axis=0)
    product_rows = jnp.transpose(product_rows, (1, 0, 2, 3)).reshape(step_x, width_y, depth)
    mine = lax.dynamic_slice_in_dim(estimate, group * step_x, step_x, axis=0)
    return lax.all_gather(mine * product_rows, "view", axis=0, tiled=True)


def solution(mesh):
    in_specs = (P("blk", None, None), P("view", "blk", None, None), P(), P(None, "blk", None))
    out_specs = P("blk", None, None)
    return jax.shard_map(local, mesh=mesh, in_specs=in_specs, out_specs=out_specs, check_vma=False)
```

profile of v0, /device:TPU:1, one launch (start us, length us, event | category | flops | bytes accessed | tf_op | source)
XLA Modules:
  0.0 175.8 jit_solution(12433264027804252495)
XLA Ops:
  6.5 1.3 convert_element_type.38
  7.9 4.0 %collective-permute-start = (bf16[4,128,128]{2,1,0:T(8,128)(2,1)S(1)}, bf16[4,128,128]{2,1,0:T(8,128)(2,1)S(1)}, u32[]{:S(2)}, u32[]{:S(2)}) collective-permute-start(bf16[4,128,128]{2,1,0:T(8,128)(2,1)S(1)} %get-tuple-element.40), channel_id=1, source_target_pairs={{0,1},{1,2},{2,3},{3,4},{4,5},{5,6},{6,7},{7,8},{8,9},{9,10},{10,1... | collective-permute-start | bytes 393224 | tf_op jit(solution)/shard_map/ppermute | solution.py:17
  11.8 1.3 collective-permute-start.1
  13.2 1.7 fusion.97
  14.8 3.2 %fusion.10 = bf16[9,7,152,128]{3,1,2,0:T(8,128)(2,1)} fusion(f32[1,9,7,25]{3,0,2,1:T(1,128)S(1)} %get-tuple-element.6, f32[]{:T(128)} %get-tuple-element.5), kind=kOutput, calls=%fused_computation.13 | convolution fusion | flops 63488080 | bytes 2457760 | tf_op jit(solution)/shard_map/abt,tpz->abpz/dot_general | solution.py:55
  18.0 1.6 iota_compare_fusion
  19.6 0.0 copy-start.1
  19.6 2.1 %copy.10 = bf16[9,7,152,128]{3,2,1,0:T(8,128)(2,1)S(1)} copy(bf16[9,7,152,128]{3,1,2,0:T(8,128)(2,1)} %fusion.10) | data formatting | bytes 4902912 | tf_op jit(solution)/shard_map/convert_element_type | solution.py:55
  21.7 0.0 copy-done.1
  21.7 0.1 fusion.75
  21.8 0.1 fusion.76
  21.9 0.1 broadcast_in_dim.28
  22.0 0.1 broadcast_in_dim.29
  22.1 0.0 collective-permute-done
  22.1 0.0 collective-permute-done.1
  22.1 2.9 %fusion.23 = bf16[24,70,152]{2,1,0:T(8,128)(2,1)S(1)} fusion(s32[]{:T(128)S(6)} %select_n.67, bf16[4,128,128]{2,1,0:T(8,128)(2,1)S(1)} %collective-permute-done, bf16[16,128,128]{2,1,0:T(8,128)(2,1)S(1)} %convert_element_type.38, pred[24,134,152]{2,1,0:T(8,128)(4,1)} %get-tuple-element.45, pred[24,134,152]{2,1,0:T(8,128)(4,1)} %get-tuple-element.46, ...), kind=kLoop, calls=%fused_computation.61 | loop fusion | flops 5873280 | bytes 1808896 | tf_op jit(solution)/shard_map/concatenate | solution.py:15
  25.0 3.1 %fusion.99 = (bf16[24,64,152]{2,1,0:T(8,128)(2,1)S(1)}, bf16[24,64,152]{2,1,0:T(8,128)(2,1)}, bf16[24,64,152]{2,1,0:T(8,128)(2,1)}, bf16[24,64,152]{2,1,0:T(8,12...) fusion(bf16[24,70,152]{2,1,0:T(8,128)(2,1)S(1)} %fusion.23), kind=kLoop, calls=%fused_computation.152 | loop fusion | bytes 6537216 | tf_op jit(solution)/shard_map/slice | solution.py:68
  28.1 8.4 %concatenate.16 = bf16[24,64,1064]{2,1,0:T(8,128)(2,1)} concatenate(bf16[24,64,152]{2,1,0:T(8,128)(2,1)} %get-tuple-element.38, bf16[24,64,152]{2,1,0:T(8,128)(2,1)} %get-tuple-element.37, bf16[24,64,152]{2,1,0:T(8,128)(2,1)} %get-tuple-element.36, bf16[24,64,152]{2,1,0:T(8,128)(2,1)} %get-tuple-element.35, bf16[24,64,152]{2,1,0:T(8,128)(2,1)} %get-tuple-element.34, ...), dimensions={2} | concatenate | bytes 6537216 | tf_op jit(solution)/shard_map/concatenate | solution.py:67
  36.5 12.6 %pad_slice_fusion.27 = (bf16[16,64,1152]{2,1,0:T(8,128)(2,1)S(1)}, bf16[16,64,1152]{2,1,0:T(8,128)(2,1)S(1)}, bf16[16,64,1152]{2,1,0:T(8,128)(2,1)S(1)}, bf16[16...) fusion(bf16[24,64,1064]{2,1,0:T(8,128)(2,1)} %concatenate.16), kind=kLoop, calls=%fused_computation.106 | loop fusion | bytes 24502272 | tf_op jit(solution)/shard_map/slice | solution.py:74
  49.1 0.8 fusion.35
  49.9 0.8 convolution_add_fusion.15
  50.7 0.8 convolution_add_fusion.14
  51.5 0.8 convolution_add_fusion.13
  52.3 0.8 convolution_add_fusion.12
  53.1 0.8 convolution_add_fusion.11
  53.9 0.8 convolution_add_fusion.10
  54.6 0.8 convolution_add_fusion.9
  55.4 0.0 copy-start
  55.4 0.8 convolution_add_fusion.8
  56.2 0.2 copy-done
  56.4 0.1 fusion.33
  56.6 1.1 collective-permute-start.2
  57.6 0.6 fusion.96
  58.3 0.1 rev.3
  58.4 0.1 collective-permute-done.2
  58.5 0.1 pad_maximum_fusion.2
  58.6 1.3 collective-permute-start.4
  59.9 4.9 %collective-permute-start.3 = (bf16[4,70,128]{2,1,0:T(8,128)(2,1)S(1)}, bf16[4,70,128]{2,1,0:T(8,128)(2,1)S(1)}, u32[]{:S(2)}, u32[]{:S(2)}) collective-permute-start(bf16[4,70,128]{2,1,0:T(8,128)(2,1)S(1)} %get-tuple-element.41), channel_id=1, source_target_pairs={{0,1},{1,2},{2,3},{3,4},{4,5},{5,6},{6,7},{7,8},{8,9},{9,10},{10,1... | collective-permute-start | bytes 215048 | tf_op jit(solution)/shard_map/ppermute | solution.py:17
  64.8 1.0 fusion.13
  65.7 0.3 copy.11
  66.1 0.0 collective-permute-done.4
  66.1 0.1 collective-permute-done.3
  66.1 0.7 select_maximum_fusion
  66.8 3.1 %fusion.98 = (bf16[24,64,152]{2,1,0:T(8,128)(2,1)S(1)}, bf16[24,64,152]{2,1,0:T(8,128)(2,1)}, bf16[24,64,152]{2,1,0:T(8,128)(2,1)}, bf16[24,64,152]{2,1,0:T(8,12...) fusion(bf16[24,70,152]{2,1,0:T(8,128)(2,1)S(1)} %select_maximum_fusion), kind=kLoop, calls=%fused_computation.151 | loop fusion | bytes 6537216 | tf_op jit(solution)/shard_map/slice | solution.py:68
  70.0 8.4 %concatenate.19 = bf16[24,64,1064]{2,1,0:T(8,128)(2,1)} concatenate(bf16[24,64,152]{2,1,0:T(8,128)(2,1)} %get-tuple-element.31, bf16[24,64,152]{2,1,0:T(8,128)(2,1)} %get-tuple-element.30, bf16[24,64,152]{2,1,0:T(8,128)(2,1)} %get-tuple-element.29, bf16[24,64,152]{2,1,0:T(8,128)(2,1)} %get-tuple-element.28, bf16[24,64,152]{2,1,0:T(8,128)(2,1)} %get-tuple-element.27, ...), dimensions={2} | concatenate | bytes 6537216 | tf_op jit(solution)/shard_map/concatenate | solution.py:67
  78.4 12.6 %pad_slice_fusion.18 = (bf16[16,64,1152]{2,1,0:T(8,128)(2,1)S(1)}, bf16[16,64,1152]{2,1,0:T(8,128)(2,1)S(1)}, bf16[16,64,1152]{2,1,0:T(8,128)(2,1)S(1)}, bf16[16...) fusion(bf16[24,64,1064]{2,1,0:T(8,128)(2,1)} %concatenate.19), kind=kLoop, calls=%fused_computation.97 | loop fusion | bytes 24502272 | tf_op jit(solution)/shard_map/slice | solution.py:74
  91.0 0.8 fusion.54
  91.8 0.8 convolution_add_fusion.7
  92.6 0.8 convolution_add_fusion.6
  93.4 0.8 convolution_add_fusion.5
  94.1 0.8 convolution_add_fusion.4
  94.9 0.8 convolution_add_fusion.3
  95.7 0.8 convolution_add_fusion.2
  96.5 0.8 convolution_add_fusion.1
  97.3 0.8 convolution_add_fusion
  98.1 0.9 broadcast_select_fusion
  99.0 9.7 %all-to-all-start = ((f32[16,1,64,128]{3,2,1,0:T(8,128)}), f32[16,1,64,128]{3,2,1,0:T(8,128)S(1)}, u32[]{:S(2)}, u32[]{:S(2)}) async-start(f32[16,1,64,128]{3,2,1,0:T(8,128)} %broadcast_select_fusion), calls=%async_computation | async-start | bytes 1048576 | tf_op jit(solution)/shard_map/all_to_all | solution.py:122
  108.7 0.0 all-gather.2.cloned.1.call-start
  108.7 17.3 %all-to-all-done = f32[16,1,64,128]{3,2,1,0:T(8,128)S(1)} async-done(((f32[16,1,64,128]{3,2,1,0:T(8,128)}), f32[16,1,64,128]{3,2,1,0:T(8,128)S(1)}, u32[]{:S(2)}, u32[]{:S(2)}) %all-to-all-start) | async-done | bytes 524320 | tf_op jit(solution)/shard_map/all_to_all | solution.py:122
  126.0 1.5 bitcast_multiply_fusion
  127.5 0.0 all-gather.2.cloned.1.call-update
  127.5 39.1 %all-gather.2.cloned.1.call-done = f32[16,128,128]{2,1,0:T(8,128)} async-done(((f32[1,128,128]{2,1,0:T(8,128)}), f32[16,128,128]{2,1,0:T(8,128)}) %all-gather.2.cloned.1.call-update) | async-done | bytes 1048592 | tf_op jit(solution)/shard_map/all_gather | solution.py:127
  166.7 2.3 %copy.26 = f32[16,128,128]{2,1,0:T(8,128)} copy(f32[16,128,128]{2,1,0:T(8,128)} %all-gather.2.cloned.1.call-done) | data formatting | bytes 2097152
  (4 shorter events, 0.1 us)
Async XLA Ops:
  7.9 14.2 %collective-permute-start = (bf16[4,128,128]{2,1,0:T(8,128)(2,1)S(1)}, bf16[4,128,128]{2,1,0:T(8,128)(2,1)S(1)}, u32[]{:S(2)}, u32[]{:S(2)}) collective-permute-start(bf16[4,128,128]{2,1,0:T(8,128)(2,1)S(1)} %get-tuple-element.40), channel_id=1, source_target_pairs={{0,1},{1,2},{2,3},{3,4},{4,5},{5,6},{6,7},{7,8},{8,9},{9,10},{10,1... | collective-permute-start | bytes 393224 | tf_op jit(solution)/shard_map/ppermute | solution.py:17
  11.8 10.3 %collective-permute-start.1 = (bf16[4,128,128]{2,1,0:T(8,128)(2,1)S(1)}, bf16[4,128,128]{2,1,0:T(8,128)(2,1)S(1)}, u32[]{:S(2)}, u32[]{:S(2)}) collective-permute-start(bf16[4,128,128]{2,1,0:T(8,128)(2,1)S(1)} %get-tuple-element.39), channel_id=1, source_target_pairs={{1,0},{2,1},{3,2},{4,3},{5,4},{6,5},{7,6},{8,7},{9,8},{10,9},{11,1... | collective-permute-start | bytes 393224 | tf_op jit(solution)/shard_map/ppermute | solution.py:19
  19.6 2.2 %copy-start.1 = (s32[8,1,4]{0,2,1:T(4,128)S(1)}, s32[8,1,4]{0,2,1:T(4,128)}, u32[]{:S(2)}) copy-start(s32[8,1,4]{0,2,1:T(4,128)} %param.7) | copy-start | bytes 388
  55.4 1.0 copy-start
  56.6 1.9 %collective-permute-start.2 = (bf16[16,3,128]{2,1,0:T(4,128)(2,1)S(1)}, bf16[16,3,128]{2,1,0:T(4,128)(2,1)S(1)}, u32[]{:S(2)}, u32[]{:S(2)}) collective-permute-start(bf16[16,3,128]{2,1,0:T(4,128)(2,1)S(1)} %slice_select_fusion), channel_id=1, source_target_pairs={{0,16},{16,0},{32,48},{48,32},{64,80},{80,64},{96,112},{112,96},{1... | collective-permute-start | bytes 36872 | tf_op jit(solution)/shard_map/ppermute | solution.py:33
  58.6 7.5 %collective-permute-start.4 = (bf16[4,70,128]{2,1,0:T(8,128)(2,1)S(1)}, bf16[4,70,128]{2,1,0:T(8,128)(2,1)S(1)}, u32[]{:S(2)}, u32[]{:S(2)}) collective-permute-start(bf16[4,70,128]{2,1,0:T(8,128)(2,1)S(1)} %get-tuple-element.42), channel_id=1, source_target_pairs={{1,0},{2,1},{3,2},{4,3},{5,4},{6,5},{7,6},{8,7},{9,8},{10,9},{11,1... | collective-permute-start | bytes 215048 | tf_op jit(solution)/shard_map/ppermute | solution.py:19
  59.9 6.3 %collective-permute-start.3 = (bf16[4,70,128]{2,1,0:T(8,128)(2,1)S(1)}, bf16[4,70,128]{2,1,0:T(8,128)(2,1)S(1)}, u32[]{:S(2)}, u32[]{:S(2)}) collective-permute-start(bf16[4,70,128]{2,1,0:T(8,128)(2,1)S(1)} %get-tuple-element.41), channel_id=1, source_target_pairs={{0,1},{1,2},{2,3},{3,4},{4,5},{5,6},{6,7},{7,8},{8,9},{9,10},{10,1... | collective-permute-start | bytes 215048 | tf_op jit(solution)/shard_map/ppermute | solution.py:17
  99.0 27.0 %all-to-all-start = ((f32[16,1,64,128]{3,2,1,0:T(8,128)}), f32[16,1,64,128]{3,2,1,0:T(8,128)S(1)}, u32[]{:S(2)}, u32[]{:S(2)}) async-start(f32[16,1,64,128]{3,2,1,0:T(8,128)} %broadcast_select_fusion), calls=%async_computation | async-start | bytes 1048576 | tf_op jit(solution)/shard_map/all_to_all | solution.py:122
  108.7 58.0 %all-gather.2.cloned.1.call-start = ((), (), s32[]{:S(2)}) async-start(), calls=%async_computation.1 | async-start | bytes 1114112 | tf_op jit(solution)/shard_map/all_gather | solution.py:127
Sparse Core Ops, SparseCore 0:
  127.7 38.9 all-gather.1
where the time goes:
time: 177 us; the launch traced here: 176 us
  waiting for transfers between devices  56.6 us (32%)
  local copies, waits for them, and re-layouts  53.6 us (30%)
  starting transfers between devices  22.2 us (13%)
  matrix products  18.2 us (10%)
  between operations  13.7 us (8%)
  other arithmetic  11.5 us (6%)
    all_gather x1, waiting for transfers between devices, local(): return lax.all_gather(mine * product_rows, 'view', axis=0, tiled=True)  39.1 us
    slice x2, local copies, waits for them, and re-layouts, convolve(): columns[shift_x:shift_x + rows_x].reshape(rows_x * rows_y, -1)  25.2 us
    all_to_all x1, waiting for transfers between devices, local(): got = lax.all_to_all(rows, 'view', 0, 0)  17.3 us
    concatenate x2, local copies, waits for them, and re-layouts, convolve(): jnp.concatenate([padded_part[:, step_y:step_y + rows_y, :] for step_y in...  16.9 us
    dot_general x18, matrix products, convolve(): jnp.dot(columns[shift_x:shift_x + rows_x].reshape(rows_x * rows_y, -1), b...  14 us
    all_to_all x1, starting transfers between devices, local(): got = lax.all_to_all(rows, 'view', 0, 0)  9.68 us
    ppermute x2, starting transfers between devices, with_halo(): lax.ppermute(tail, axis, [(i, (i + 1) % count) for i in range(ends)])  8.85 us
    slice x2, local copies, waits for them, and re-layouts, convolve(): padded_part[:, step_y:step_y + rows_y, :]  6.25 us
  transfers between devices with their start and end apart: 7, of which 4 were waited for; matrix products, arithmetic and copies ran while one was open for 6% of the time, Pallas kernels for 0%

commit v1 on v0

--- a/solution.py
+++ b/solution.py
@@ -1,9 +1,21 @@
+import functools
 import jax
 import jax.numpy as jnp
 from jax import lax
 from jax.sharding import PartitionSpec as P
 
 BY = 32
+
+
+def return_all_the_body(matrix, dim_i):
+    rack = []
+    for _ in range(lax.axis_size("view")):
+        rack.append(matrix)
+    extra = jnp.concatenate(lax.all_to_all(jnp.stack(rack), "view", 0, 0), dim_i)
+    return extra
+
+
+body_watch = functools.partial(return_all_the_body, dim_i=0)
 
 
 def with_halo(cells, sides, width):
@@ -124,7 +136,7 @@
     product_rows = jnp.prod(got, axis=0)
     product_rows = jnp.transpose(product_rows, (1, 0, 2, 3)).reshape(step_x, width_y, depth)
     mine = lax.dynamic_slice_in_dim(estimate, group * step_x, step_x, axis=0)
-    return lax.all_gather(mine * product_rows, "view", axis=0, tiled=True)
+    return body_watch(mine * product_rows)
 
 
 def solution(mesh):

time: 177 us -> 158 us (0.89)
  the two profiles are of different devices: /device:TPU:1 before, /device:TPU:25 now
where the time goes in v1:
time: 158 us; the launch traced here: 157 us
  local copies, waits for them, and re-layouts  51.4 us (33%)
  blocking collectives  31.3 us (20%)
  starting transfers between devices  24.3 us (15%)
  waiting for transfers between devices  20.4 us (13%)
  matrix products  18.2 us (12%)
  other arithmetic  10.9 us (7%)
    all_to_all x1, blocking collectives, return_all_the_body(): lax.all_to_all(jnp.stack(rack), 'view', 0, 0)  31.3 us
    slice x2, local copies, waits for them, and re-layouts, convolve(): columns[shift_x:shift_x + rows_x].reshape(rows_x * rows_y, -1)  24.2 us
    all_to_all x1, waiting for transfers between devices, local(): got = lax.all_to_all(rows, 'view', 0, 0)  17.3 us
    concatenate x2, local copies, waits for them, and re-layouts, convolve(): jnp.concatenate([padded_part[:, step_y:step_y + rows_y, :] for step_y in...  16.9 us
    dot_general x18, matrix products, convolve(): jnp.dot(columns[shift_x:shift_x + rows_x].reshape(rows_x * rows_y, -1), b...  14 us
    all_to_all x1, starting transfers between devices, local(): got = lax.all_to_all(rows, 'view', 0, 0)  10.3 us
    ppermute x2, starting transfers between devices, with_halo(): lax.ppermute(head, axis, [((i + 1) % count, i) for i in range(ends)])  6.73 us
    slice x2, local copies, waits for them, and re-layouts, convolve(): padded_part[:, step_y:step_y + rows_y, :]  6.24 us
  transfers between devices with their start and end apart: 6, of which 3 were waited for; matrix products, arithmetic and copies ran while one was open for 7% of the time, Pallas kernels for 0%

profile of v1, /device:TPU:25, one launch (start us, length us, event | category | flops | bytes accessed | tf_op | source)
XLA Modules:
  0.0 156.8 jit_solution(3442602763010382013)
XLA Ops:
  0.0 1.3 convert_element_type.38
  1.3 3.1 %collective-permute-start = (bf16[4,128,128]{2,1,0:T(8,128)(2,1)S(1)}, bf16[4,128,128]{2,1,0:T(8,128)(2,1)S(1)}, u32[]{:S(2)}, u32[]{:S(2)}) collective-permute-start(bf16[4,128,128]{2,1,0:T(8,128)(2,1)S(1)} %get-tuple-element.40), channel_id=1, source_target_pairs={{0,1},{1,2},{2,3},{3,4},{4,5},{5,6},{6,7},{7,8},{8,9},{9,10},{10,1... | collective-permute-start | bytes 393224 | tf_op jit(solution)/shard_map/ppermute | solution.py:29
  4.5 4.3 %collective-permute-start.1 = (bf16[4,128,128]{2,1,0:T(8,128)(2,1)S(1)}, bf16[4,128,128]{2,1,0:T(8,128)(2,1)S(1)}, u32[]{:S(2)}, u32[]{:S(2)}) collective-permute-start(bf16[4,128,128]{2,1,0:T(8,128)(2,1)S(1)} %get-tuple-element.39), channel_id=1, source_target_pairs={{1,0},{2,1},{3,2},{4,3},{5,4},{6,5},{7,6},{8,7},{9,8},{10,9},{11,1... | collective-permute-start | bytes 393224 | tf_op jit(solution)/shard_map/ppermute | solution.py:31
  8.8 1.7 %fusion.98 = (f32[]{:T(128)}, f32[1,9,7,25]{3,0,2,1:T(1,128)S(1)}) fusion(f32[8,9,7,25]{3,0,2,1:T(8,128)} %param.6, s32[]{:T(128)S(6)} %select_n.62), kind=kLoop, calls=%fused_computation.151 | loop fusion | flops 1574 | bytes 12608 | tf_op jit(solution)/shard_map/reduce_sum | solution.py:109
  10.4 3.2 %fusion.10 = bf16[9,7,152,128]{3,1,2,0:T(8,128)(2,1)} fusion(f32[1,9,7,25]{3,0,2,1:T(1,128)S(1)} %get-tuple-element.6, f32[]{:T(128)} %get-tuple-element.5), kind=kOutput, calls=%fused_computation.13 | convolution fusion | flops 63488080 | bytes 2457760 | tf_op jit(solution)/shard_map/abt,tpz->abpz/dot_general | solution.py:67
  13.6 1.6 %iota_compare_fusion = (pred[24,134,152]{2,1,0:T(8,128)(4,1)}, pred[24,134,152]{2,1,0:T(8,128)(4,1)}) fusion(), kind=kLoop, calls=%fused_computation | loop fusion | flops 977664 | bytes 977664 | tf_op jit(solution)/shard_map/jit(_pad)/pad | solution.py:107
  15.2 0.0 copy-start.1
  15.2 2.1 %copy.10 = bf16[9,7,152,128]{3,2,1,0:T(8,128)(2,1)S(1)} copy(bf16[9,7,152,128]{3,1,2,0:T(8,128)(2,1)} %fusion.10) | data formatting | bytes 4902912 | tf_op jit(solution)/shard_map/convert_element_type | solution.py:67
  17.3 0.0 copy-done.1
  17.3 0.1 fusion.76
  17.4 0.1 fusion.77
  17.5 0.1 broadcast_in_dim.28
  17.6 0.1 broadcast_in_dim.29
  17.7 0.0 collective-permute-done
  17.7 0.0 collective-permute-done.1
  17.7 2.9 %fusion.23 = bf16[24,70,152]{2,1,0:T(8,128)(2,1)S(1)} fusion(s32[]{:T(128)S(6)} %select_n.67, bf16[4,128,128]{2,1,0:T(8,128)(2,1)S(1)} %collective-permute-done, bf16[16,128,128]{2,1,0:T(8,128)(2,1)S(1)} %convert_element_type.38, pred[24,134,152]{2,1,0:T(8,128)(4,1)} %get-tuple-element.45, pred[24,134,152]{2,1,0:T(8,128)(4,1)} %get-tuple-element.46, ...), kind=kLoop, calls=%fused_computation.61 | loop fusion | flops 5873280 | bytes 1808896 | tf_op jit(solution)/shard_map/concatenate | solution.py:27
  20.6 3.1 %fusion.100 = (bf16[24,64,152]{2,1,0:T(8,128)(2,1)S(1)}, bf16[24,64,152]{2,1,0:T(8,128)(2,1)}, bf16[24,64,152]{2,1,0:T(8,128)(2,1)}, bf16[24,64,152]{2,1,0:T(8,1...) fusion(bf16[24,70,152]{2,1,0:T(8,128)(2,1)S(1)} %fusion.23), kind=kLoop, calls=%fused_computation.153 | loop fusion | bytes 6537216 | tf_op jit(solution)/shard_map/slice | solution.py:80
  23.7 8.4 %concatenate.16 = bf16[24,64,1064]{2,1,0:T(8,128)(2,1)} concatenate(bf16[24,64,152]{2,1,0:T(8,128)(2,1)} %get-tuple-element.38, bf16[24,64,152]{2,1,0:T(8,128)(2,1)} %get-tuple-element.37, bf16[24,64,152]{2,1,0:T(8,128)(2,1)} %get-tuple-element.36, bf16[24,64,152]{2,1,0:T(8,128)(2,1)} %get-tuple-element.35, bf16[24,64,152]{2,1,0:T(8,128)(2,1)} %get-tuple-element.34, ...), dimensions={2} | concatenate | bytes 6537216 | tf_op jit(solution)/shard_map/concatenate | solution.py:79
  32.2 12.1 %pad_slice_fusion.27 = (bf16[16,64,1152]{2,1,0:T(8,128)(2,1)S(1)}, bf16[16,64,1152]{2,1,0:T(8,128)(2,1)S(1)}, bf16[16,64,1152]{2,1,0:T(8,128)(2,1)S(1)}, bf16[16...) fusion(bf16[24,64,1064]{2,1,0:T(8,128)(2,1)} %concatenate.16), kind=kLoop, calls=%fused_computation.106 | loop fusion | bytes 24502272 | tf_op jit(solution)/shard_map/slice | solution.py:86
  44.3 0.8 fusion.35
  45.1 0.8 convolution_add_fusion.15
  45.9 0.8 convolution_add_fusion.14
  46.6 0.8 convolution_add_fusion.13
  47.4 0.8 convolution_add_fusion.12
  48.2 0.8 convolution_add_fusion.11
  49.0 0.8 convolution_add_fusion.10
  49.8 0.8 convolution_add_fusion.9
  50.6 0.0 copy-start
  50.6 0.8 convolution_add_fusion.8
  51.4 0.2 copy-done
  51.5 0.1 fusion.33
  51.7 1.4 collective-permute-start.2
  53.0 0.6 fusion.97
  53.7 0.1 rev.3
  53.8 0.1 collective-permute-done.2
  53.9 0.1 pad_maximum_fusion.2
  54.0 2.5 %collective-permute-start.4 = (bf16[4,70,128]{2,1,0:T(8,128)(2,1)S(1)}, bf16[4,70,128]{2,1,0:T(8,128)(2,1)S(1)}, u32[]{:S(2)}, u32[]{:S(2)}) collective-permute-start(bf16[4,70,128]{2,1,0:T(8,128)(2,1)S(1)} %get-tuple-element.42), channel_id=1, source_target_pairs={{1,0},{2,1},{3,2},{4,3},{5,4},{6,5},{7,6},{8,7},{9,8},{10,9},{11,1... | collective-permute-start | bytes 215048 | tf_op jit(solution)/shard_map/ppermute | solution.py:31
  56.4 2.8 %collective-permute-start.3 = (bf16[4,70,128]{2,1,0:T(8,128)(2,1)S(1)}, bf16[4,70,128]{2,1,0:T(8,128)(2,1)S(1)}, u32[]{:S(2)}, u32[]{:S(2)}) collective-permute-start(bf16[4,70,128]{2,1,0:T(8,128)(2,1)S(1)} %get-tuple-element.41), channel_id=1, source_target_pairs={{0,1},{1,2},{2,3},{3,4},{4,5},{5,6},{6,7},{7,8},{8,9},{9,10},{10,1... | collective-permute-start | bytes 215048 | tf_op jit(solution)/shard_map/ppermute | solution.py:29
  59.3 1.0 fusion.13
  60.2 0.3 copy.11
  60.6 0.0 collective-permute-done.4
  60.6 3.0 %collective-permute-done.3 = bf16[4,70,128]{2,1,0:T(8,128)(2,1)S(1)} collective-permute-done((bf16[4,70,128]{2,1,0:T(8,128)(2,1)S(1)}, bf16[4,70,128]{2,1,0:T(8,128)(2,1)S(1)}, u32[]{:S(2)}, u32[]{:S(2)}) %collective-permute-start.3) | collective-permute-done | bytes 71712 | tf_op jit(solution)/shard_map/ppermute | solution.py:29
  63.6 0.7 select_maximum_fusion
  64.3 3.1 %fusion.99 = (bf16[24,64,152]{2,1,0:T(8,128)(2,1)S(1)}, bf16[24,64,152]{2,1,0:T(8,128)(2,1)}, bf16[24,64,152]{2,1,0:T(8,128)(2,1)}, bf16[24,64,152]{2,1,0:T(8,12...) fusion(bf16[24,70,152]{2,1,0:T(8,128)(2,1)S(1)} %select_maximum_fusion), kind=kLoop, calls=%fused_computation.152 | loop fusion | bytes 6537216 | tf_op jit(solution)/shard_map/slice | solution.py:80
  67.5 8.5 %concatenate.19 = bf16[24,64,1064]{2,1,0:T(8,128)(2,1)} concatenate(bf16[24,64,152]{2,1,0:T(8,128)(2,1)} %get-tuple-element.31, bf16[24,64,152]{2,1,0:T(8,128)(2,1)} %get-tuple-element.30, bf16[24,64,152]{2,1,0:T(8,128)(2,1)} %get-tuple-element.29, bf16[24,64,152]{2,1,0:T(8,128)(2,1)} %get-tuple-element.28, bf16[24,64,152]{2,1,0:T(8,128)(2,1)} %get-tuple-element.27, ...), dimensions={2} | concatenate | bytes 6537216 | tf_op jit(solution)/shard_map/concatenate | solution.py:79
  75.9 12.1 %pad_slice_fusion.18 = (bf16[16,64,1152]{2,1,0:T(8,128)(2,1)S(1)}, bf16[16,64,1152]{2,1,0:T(8,128)(2,1)S(1)}, bf16[16,64,1152]{2,1,0:T(8,128)(2,1)S(1)}, bf16[16...) fusion(bf16[24,64,1064]{2,1,0:T(8,128)(2,1)} %concatenate.19), kind=kLoop, calls=%fused_computation.97 | loop fusion | bytes 24502272 | tf_op jit(solution)/shard_map/slice | solution.py:86
  88.0 0.8 fusion.54
  88.8 0.8 convolution_add_fusion.7
  89.6 0.8 convolution_add_fusion.6
  90.4 0.8 convolution_add_fusion.5
  91.2 0.8 convolution_add_fusion.4
  92.0 0.8 convolution_add_fusion.3
  92.7 0.8 convolution_add_fusion.2
  93.5 0.8 convolution_add_fusion.1
  94.3 0.8 convolution_add_fusion
  95.1 0.9 broadcast_select_fusion
  96.0 10.3 %all-to-all-start = ((f32[16,1,64,128]{3,2,1,0:T(8,128)}), f32[16,1,64,128]{3,2,1,0:T(8,128)S(1)}, u32[]{:S(2)}, u32[]{:S(2)}) async-start(f32[16,1,64,128]{3,2,1,0:T(8,128)} %broadcast_select_fusion), calls=%async_computation | async-start | bytes 1048576 | tf_op jit(solution)/shard_map/all_to_all | solution.py:134
  106.3 17.3 %all-to-all-done = f32[16,1,64,128]{3,2,1,0:T(8,128)S(1)} async-done(((f32[16,1,64,128]{3,2,1,0:T(8,128)}), f32[16,1,64,128]{3,2,1,0:T(8,128)S(1)}, u32[]{:S(2)}, u32[]{:S(2)}) %all-to-all-start) | async-done | bytes 524320 | tf_op jit(solution)/shard_map/all_to_all | solution.py:134
  123.6 0.9 fusion.72
  124.5 0.1 stack.2
  124.6 31.3 %all_to_all.10 = f32[16,1,128,128]{3,2,1,0:T(8,128)S(1)} all-to-all(f32[16,1,128,128]{3,2,1,0:T(8,128)S(1)} %stack.2), channel_id=1, replica_groups=mesh['view'=16,'blk'=16] {'view'}, dimensions={0} | all-to-all | bytes 2097152 | tf_op jit(solution)/shard_map/all_to_all | solution.py:14
  155.8 1.0 copy.26
  (4 shorter events, 0.1 us)
Async XLA Ops:
  1.3 16.4 %collective-permute-start = (bf16[4,128,128]{2,1,0:T(8,128)(2,1)S(1)}, bf16[4,128,128]{2,1,0:T(8,128)(2,1)S(1)}, u32[]{:S(2)}, u32[]{:S(2)}) collective-permute-start(bf16[4,128,128]{2,1,0:T(8,128)(2,1)S(1)} %get-tuple-element.40), channel_id=1, source_target_pairs={{0,1},{1,2},{2,3},{3,4},{4,5},{5,6},{6,7},{7,8},{8,9},{9,10},{10,1... | collective-permute-start | bytes 393224 | tf_op jit(solution)/shard_map/ppermute | solution.py:29
  4.5 13.2 %collective-permute-start.1 = (bf16[4,128,128]{2,1,0:T(8,128)(2,1)S(1)}, bf16[4,128,128]{2,1,0:T(8,128)(2,1)S(1)}, u32[]{:S(2)}, u32[]{:S(2)}) collective-permute-start(bf16[4,128,128]{2,1,0:T(8,128)(2,1)S(1)} %get-tuple-element.39), channel_id=1, source_target_pairs={{1,0},{2,1},{3,2},{4,3},{5,4},{6,5},{7,6},{8,7},{9,8},{10,9},{11,1... | collective-permute-start | bytes 393224 | tf_op jit(solution)/shard_map/ppermute | solution.py:31
  15.2 2.2 %copy-start.1 = (s32[8,1,4]{0,2,1:T(4,128)S(1)}, s32[8,1,4]{0,2,1:T(4,128)}, u32[]{:S(2)}) copy-start(s32[8,1,4]{0,2,1:T(4,128)} %param.7) | copy-start | bytes 388
  50.6 1.0 copy-start
  51.7 2.2 %collective-permute-start.2 = (bf16[16,3,128]{2,1,0:T(4,128)(2,1)S(1)}, bf16[16,3,128]{2,1,0:T(4,128)(2,1)S(1)}, u32[]{:S(2)}, u32[]{:S(2)}) collective-permute-start(bf16[16,3,128]{2,1,0:T(4,128)(2,1)S(1)} %slice_select_fusion), channel_id=1, source_target_pairs={{0,16},{16,0},{32,48},{48,32},{64,80},{80,64},{96,112},{112,96},{1... | collective-permute-start | bytes 36872 | tf_op jit(solution)/shard_map/ppermute | solution.py:45
  54.0 6.6 %collective-permute-start.4 = (bf16[4,70,128]{2,1,0:T(8,128)(2,1)S(1)}, bf16[4,70,128]{2,1,0:T(8,128)(2,1)S(1)}, u32[]{:S(2)}, u32[]{:S(2)}) collective-permute-start(bf16[4,70,128]{2,1,0:T(8,128)(2,1)S(1)} %get-tuple-element.42), channel_id=1, source_target_pairs={{1,0},{2,1},{3,2},{4,3},{5,4},{6,5},{7,6},{8,7},{9,8},{10,9},{11,1... | collective-permute-start | bytes 215048 | tf_op jit(solution)/shard_map/ppermute | solution.py:31
  56.4 7.2 %collective-permute-start.3 = (bf16[4,70,128]{2,1,0:T(8,128)(2,1)S(1)}, bf16[4,70,128]{2,1,0:T(8,128)(2,1)S(1)}, u32[]{:S(2)}, u32[]{:S(2)}) collective-permute-start(bf16[4,70,128]{2,1,0:T(8,128)(2,1)S(1)} %get-tuple-element.41), channel_id=1, source_target_pairs={{0,1},{1,2},{2,3},{3,4},{4,5},{5,6},{6,7},{7,8},{8,9},{9,10},{10,1... | collective-permute-start | bytes 215048 | tf_op jit(solution)/shard_map/ppermute | solution.py:29
  96.0 27.6 %all-to-all-start = ((f32[16,1,64,128]{3,2,1,0:T(8,128)}), f32[16,1,64,128]{3,2,1,0:T(8,128)S(1)}, u32[]{:S(2)}, u32[]{:S(2)}) async-start(f32[16,1,64,128]{3,2,1,0:T(8,128)} %broadcast_select_fusion), calls=%async_computation | async-start | bytes 1048576 | tf_op jit(solution)/shard_map/all_to_all | solution.py:134
